TPU v7x, 32 devices: a whole 2x2x4 slice. The times are simulated.
32 devices in a mesh: dp: 16 (over z, x, core), mp: 2 (over y).
Axes of the slice: x: 2, y: 2, z: 4, core: 2. Of those that a mesh axis runs over, the one named last changes fastest.
Arguments:
- features: bfloat16 [2048, 512], P('dp'), may hold values from -6 to 6
- w_in: bfloat16 [512, 512], P(None, 'mp'), may hold values from -0.25 to 0.25
- b_in: float32 [512], P('mp'), may hold values from -1 to 1
- w_out: bfloat16 [512, 128], P('mp'), may hold values from -0.25 to 0.25
- partner: int32 [2048], P('dp'), may hold values from 0 to 2047, as said below
- window: int32 [16], replicated, may hold values from 0 to 3
Outputs:
- row_loss: float32 [512], P('dp')
- grad_w_in: float32 [512, 512], P(None, 'mp')
- grad_b_in: float32 [512], P('mp')
- grad_w_out: float32 [512, 128], P('mp')
Inputs may be any that keep to these rules, and one draw needn't show every extreme that they name: partner pairs the rows: partner[partner[i]] = i and partner[i] != i for every row i.
All inputs are finite; a program needn't handle non-finite values.
Results may differ from a plain program's by a relative error of at most 0.0027.
Values may be sent and summed in bfloat16 or wider, within the bound.
A program may use at most 64 MiB of HBM per device.

v0:
```python
import math
import jax
import jax.numpy as jnp
from jax import lax
from jax.sharding import PartitionSpec as P

A_DEV = 32
INV_TEMP = 10.0
SHIFT = 10.0
EPS = 1e-06


def contract_rows(left, right):
    return lax.dot_general(
        left, right, (((0,), (0,)), ((), ())), preferred_element_type=jnp.float32
    )


def on_device(features, w_in, b_in, w_out, partner, window):
    rows = features.shape[0]
    parts = lax.axis_size("mp")
    part = lax.axis_index("mp")
    shards = lax.axis_size("dp")
    shard = lax.axis_index("dp")
    width = rows // parts
    anchor_rows = A_DEV
    anchor_all = anchor_rows * shards
    pre = jnp.dot(features, w_in, preferred_element_type=jnp.float32) + b_in
    hidden = jax.nn.silu(pre).astype(jnp.bfloat16)
    proj = lax.psum(jnp.dot(hidden, w_out, preferred_element_type=jnp.float32), "mp")
    norm = jnp.sqrt(jnp.sum(proj * proj, axis=1, keepdims=True) + EPS)
    emb = (proj / norm).astype(jnp.bfloat16)
    embed = emb.shape[1]
    own_cols = lax.dynamic_slice_in_dim(emb, part * width, width, 0)
    columns = lax.all_gather(own_cols, "dp", axis=0, tiled=True)
    col_total = columns.shape[0]
    shard_ids = jnp.arange(shards, dtype=jnp.int32)
    my_block = jnp.sum(jnp.where(shard_ids == shard, window, 0))
    my_start = my_block * anchor_rows
    anchors = lax.dynamic_slice_in_dim(emb, my_start, anchor_rows, 0)
    anchor_partner = lax.dynamic_slice_in_dim(partner, my_start, anchor_rows, 0)
    anchor_ids = shard * rows + my_start + jnp.arange(anchor_rows, dtype=jnp.int32)

    def column_ids(start, count):
        local = start + jnp.arange(count, dtype=jnp.int32)
        return local // width * rows + part * width + local % width

    blk = math.gcd(col_total, 2048)
    nblk = col_total // blk
    col_blocks = columns.reshape(nblk, blk, embed)
    starts = jnp.arange(nblk, dtype=jnp.int32) * blk

    def forward(carry, item):
        total, hit = carry
        block, start = item
        s = jnp.dot(anchors, block.T, preferred_element_type=jnp.float32) * INV_TEMP
        ids = column_ids(start, blk)
        ex = jnp.where(ids[None, :] == anchor_ids[:, None], 0.0, jnp.exp(s - SHIFT))
        hit = hit + jnp.sum(jnp.where(ids[None, :] == anchor_partner[:, None], s, 0.0), axis=1)
        return ((total + jnp.sum(ex, axis=1), hit), None)

    zero_rows = jnp.zeros((anchor_rows,), jnp.float32)
    (total, hit), _ = lax.scan(forward, (zero_rows, zero_rows), (col_blocks, starts))
    total, hit = lax.psum((total, hit), "mp")
    row_loss = jnp.log(total) + SHIFT - hit

    def row_weights(s, ids):
        prob = jnp.where(
            ids[None, :] == anchor_ids[:, None], 0.0, jnp.exp(s - SHIFT) / total[:, None]
        )
        onehot = (ids[None, :] == anchor_partner[:, None]).astype(jnp.float32)
        return (prob - onehot).astype(jnp.bfloat16)

    def backward(acc, item):
        block, start = item
        s = jnp.dot(anchors, block.T, preferred_element_type=jnp.float32) * INV_TEMP
        weights = row_weights(s, column_ids(start, blk))
        return (acc + jnp.dot(weights, block, preferred_element_type=jnp.float32), None)

    row_part, _ = lax.scan(
        backward, jnp.zeros((anchor_rows, embed), jnp.float32), (col_blocks, starts)
    )
    totals = lax.all_gather(total, "dp", axis=0, tiled=True)
    own_ids = shard * rows + part * width + jnp.arange(width, dtype=jnp.int32)
    own_partner = lax.dynamic_slice_in_dim(partner, part * width, width, 0)
    piece = lax.all_gather(anchors, "dp", axis=0, tiled=True)
    count = piece.shape[0]
    inner = math.gcd(count, 2048)
    sub_pieces = piece.reshape(count // inner, inner, embed)
    offsets = jnp.arange(count // inner, dtype=jnp.int32) * inner

    def one_block(inner_acc, item):
        block, offset = item
        block_totals = lax.dynamic_slice_in_dim(totals, offset, inner, 0)
        flat = offset + jnp.arange(inner, dtype=jnp.int32)
        owner = flat // anchor_rows
        owner_block = jnp.sum(
            jnp.where(owner[:, None] == shard_ids[None, :], window[None, :], 0), axis=1
        )
        ids = owner * rows + owner_block * anchor_rows + flat % anchor_rows
        s = jnp.dot(own_cols, block.T, preferred_element_type=jnp.float32) * INV_TEMP
        prob = jnp.where(
            ids[None, :] == own_ids[:, None], 0.0, jnp.exp(s - SHIFT) / block_totals[None, :]
        )
        onehot = (ids[None, :] == own_partner[:, None]).astype(jnp.float32)
        weights = (prob - onehot).astype(jnp.bfloat16)
        return (inner_acc + jnp.dot(weights, block, preferred_element_type=jnp.float32), None)

    result, _ = lax.scan(one_block, jnp.zeros((width, embed), jnp.float32), (sub_pieces, offsets))
    placed = lax.dynamic_update_slice_in_dim(
        jnp.zeros((rows, embed), jnp.float32), result, part * width, 0
    )
    row_placed = lax.dynamic_update_slice_in_dim(
        jnp.zeros((rows, embed), jnp.float32), row_part, my_start, 0
    )
    grad_emb = lax.psum(row_placed + placed, "mp") * (INV_TEMP / anchor_all)
    unit = proj / norm
    grad_proj = ((grad_emb - unit * jnp.sum(unit * grad_emb, axis=1, keepdims=True)) / norm).astype(
        jnp.bfloat16
    )
    grad_w_out = contract_rows(hidden, grad_proj)
    grad_hidden = lax.dot_general(
        grad_proj, w_out, (((1,), (1,)), ((), ())), preferred_element_type=jnp.float32
    )
    sig = jax.nn.sigmoid(pre)
    grad_pre = (grad_hidden * sig * (1.0 + pre * (1.0 - sig))).astype(jnp.bfloat16)
    grad_w_in = contract_rows(features, grad_pre)
    grad_b_in = jnp.sum(grad_pre.astype(jnp.float32), axis=0)
    grad_w_in, grad_b_in, grad_w_out = lax.psum((grad_w_in, grad_b_in, grad_w_out), "dp")
    return (row_loss, grad_w_in, grad_b_in, grad_w_out)


def solution(mesh):
    return jax.shard_map(
        on_device,
        mesh=mesh,
        in_specs=(P("dp", None), P(None, "mp"), P("mp"), P("mp", None), P("dp"), P()),
        out_specs=(P("dp"), P(None, "mp"), P("mp"), P("mp", None)),
        check_vma=False,
    )
```

profile of v0, /device:TPU:0, one launch (start us, length us, event | category | flops | bytes accessed | tf_op | source)
XLA Modules:
  0.0 234.8 jit_solution(11536599049466594532)
XLA Ops:
  7.2 0.0 copy-start
  7.2 0.0 copy-start.6
  7.2 0.0 all-reduce.7.cloned.1.call-start
  7.2 0.9 copy-done
  8.1 1.1 multiply_convert_fusion
  9.2 0.0 copy-done.6
  9.3 0.8 fusion.57
  10.0 0.0 all-reduce.7.cloned.1.call-update
  10.1 0.0 all-reduce.9.cloned.1.call-start
  10.1 0.0 copy-start.7
  10.1 0.6 copy-done.7
  10.8 0.6 fusion.50
  12.1 0.0 copy-start.8
  12.1 0.6 copy-done.8
  12.8 0.1 dynamic_slice.31
  12.8 0.1 dynamic_slice.32
  12.9 0.1 select_reduce_fusion
  13.0 0.0 copy-start.9
  13.0 0.6 copy-done.9
  13.7 0.6 dynamic-slice.3
  14.9 19.6 %all-reduce.7.cloned.1.call-done = f32[128,128]{1,0:T(8,128)} async-done(((f32[128,128]{1,0:T(8,128)}), f32[128,128]{1,0:T(8,128)}) %all-reduce.7.cloned.1.call-update) | async-done | bytes 65552 | tf_op jit(solution)/shard_map/psum | solution.py:30
  34.5 0.0 copy-start.1
  34.5 1.0 multiply_reduce_fusion.1
  35.6 0.0 copy-done.1
  35.6 0.1 fusion.56
  35.7 21.7 %all_gather.10 = bf16[512,128]{1,0:T(8,128)(2,1)S(1)} all-gather(bf16[32,128]{1,0:T(8,128)(2,1)S(1)} %constant_dynamic-slice_fusion.1), channel_id=1, replica_groups=mesh['dp'=16,'mp'=2] {'dp'}, dimensions={0}, use_global_device_ids=true | all-gather | bytes 139264 | tf_op jit(solution)/shard_map/all_gather | solution.py:86
  57.4 18.1 %all_gather.9 = bf16[1024,128]{1,0:T(8,128)(2,1)S(1)} all-gather(bf16[64,128]{1,0:T(8,128)(2,1)S(1)} %constant_dynamic-slice_fusion), channel_id=1, replica_groups=mesh['dp'=16,'mp'=2] {'dp'}, dimensions={0}, use_global_device_ids=true | all-gather | bytes 278528 | tf_op jit(solution)/shard_map/all_gather | solution.py:35
  75.5 0.3 fusion.11
  75.8 4.9 %all-reduce.2 = (f32[32]{0:T(128)S(1)}, f32[32]{0:T(128)S(1)}) all-reduce(f32[32]{0:T(128)S(1)} %get-tuple-element.70, f32[32]{0:T(128)S(1)} %get-tuple-element.69), channel_id=1, replica_groups=mesh['dp'=16,'mp'=2] {'mp'}, use_global_device_ids=true, to_apply=%region_6.7 | all-reduce | flops 64 | bytes 512 | tf_op jit(solution)/shard_map/psum | solution.py:64
  80.8 0.2 dynamic-update-slice.1
  81.0 29.9 %all-reduce = f32[512]{0:T(512)S(1)} all-reduce(f32[512]{0:T(512)S(1)} %dynamic-update-slice.1), channel_id=1, replica_groups=mesh['dp'=16,'mp'=2] {'dp'}, use_global_device_ids=true, to_apply=%add | all-reduce | flops 512 | bytes 4096
  110.9 0.2 convolution_dynamic-update-slice_fusion
  111.1 0.3 fusion.10
  111.4 0.0 copy-start.3
  111.5 0.6 copy-done.3
  112.1 0.0 all-reduce.9.cloned.1.call-update
  112.1 0.0 all-reduce.11.cloned.1.call-start
  112.2 17.4 %all-reduce.9.cloned.1.call-done = f32[128,128]{1,0:T(8,128)} async-done(((f32[128,128]{1,0:T(8,128)}), f32[128,128]{1,0:T(8,128)}) %all-reduce.9.cloned.1.call-update) | async-done | bytes 65552 | tf_op jit(solution)/shard_map/psum | solution.py:116
  129.6 0.0 copy-start.2
  129.6 1.1 multiply_reduce_fusion
  130.6 0.0 copy-done.2
  130.7 0.1 divide_convert_fusion
  130.8 0.9 fusion.58
  131.6 0.0 copy-start.5
  131.6 0.2 convert_reduce_fusion
  131.8 0.7 copy-done.5
  132.5 1.0 convolution_bitcast_fusion
  133.6 0.0 all-reduce.11.cloned.1.call-update
  133.6 0.5 add_subtract_fusion
  134.1 33.6 %psum.54 = f32[256]{0:T(256)} all-reduce(f32[256]{0:T(256)S(1)} %get-tuple-element.87), channel_id=1, replica_groups=mesh['dp'=16,'mp'=2] {'dp'}, use_global_device_ids=true, to_apply=%region_12.13 | all-reduce | flops 256 | bytes 2048 | tf_op jit(solution)/shard_map/psum | solution.py:129
  167.7 57.9 %all-reduce.11.cloned.1.call-done = (f32[512,256]{0,1:T(8,128)}, f32[256,128]{1,0:T(8,128)}) async-done(((f32[512,256]{0,1:T(8,128)}, f32[256,128]{1,0:T(8,128)}), (f32[512,256]{0,1:T(8,128)}, f32[256,128]{1,0:T(8,128)})) %all-reduce.11.cloned.1.call-update) | async-done | bytes 655376 | tf_op jit(solution)/shard_map/psum | solution.py:129
  225.5 0.0 copy-start.4
  225.5 2.1 copy.11
  227.6 0.0 copy-done.4
  227.6 0.7 copy.19
  (10 shorter events, 0.1 us)
Async XLA Ops:
  7.2 1.0 copy-start
  7.2 2.1 copy-start.6
  7.2 27.3 %all-reduce.7.cloned.1.call-start = ((), (), s32[]{:S(2)}) async-start(), calls=%async_computation | async-start | bytes 131072 | tf_op jit(solution)/shard_map/psum | solution.py:30
  10.1 119.5 %all-reduce.9.cloned.1.call-start = ((), (), s32[]{:S(2)}) async-start(), calls=%async_computation.1 | async-start | bytes 131072 | tf_op jit(solution)/shard_map/psum | solution.py:116
  10.1 0.7 copy-start.7
  12.1 0.7 copy-start.8
  13.0 0.7 copy-start.9
  34.5 1.0 copy-start.1
  111.4 0.6 copy-start.3
  112.1 113.4 %all-reduce.11.cloned.1.call-start = ((), (), s32[]{:S(2)}) async-start(), calls=%async_computation.2 | async-start | bytes 1310720 | tf_op jit(solution)/shard_map/psum | solution.py:129
  129.6 1.1 copy-start.2
  131.6 0.9 copy-start.5
  225.5 2.1 copy-start.4
Sparse Core Ops, SparseCore 0:
  10.8 23.6 all-reduce.6
  112.2 17.2 all-reduce.8
  133.7 91.7 all-reduce.10
where the time goes:
time: 235 us
  blocking collectives  108 us (46%)
  waiting for transfers between devices  94.9 us (40%)
  between operations  15.3 us (7%)
  local copies, waits for them, and re-layouts  7.86 us (3%)
  matrix products  4.84 us (2%)
  other arithmetic  3.56 us (2%)
    psum x1, waiting for transfers between devices, on_device(): lax.psum((grad_w_in, grad_b_in, grad_w_out), 'dp')  57.9 us
    psum x1, blocking collectives, on_device(): lax.psum((grad_w_in, grad_b_in, grad_w_out), 'dp')  33.6 us
    unnamed x1, blocking collectives  29.9 us
    all_gather x1, blocking collectives, on_device(): piece = lax.all_gather(anchors, 'dp', axis=0, tiled=True)  21.7 us
    psum x1, waiting for transfers between devices, on_device(): lax.psum(jnp.dot(hidden, w_out, preferred_element_type=jnp.float32), 'mp')  19.6 us
    all_gather x1, blocking collectives, on_device(): columns = lax.all_gather(own_cols, 'dp', axis=0, tiled=True)  18.1 us
    psum x1, waiting for transfers between devices, on_device(): grad_emb = lax.psum(row_placed + placed, 'mp') * (INV_TEMP / anchor_all)  17.4 us
    unnamed x25, local copies, waits for them, and re-layouts  7.68 us
  transfers between devices with their start and end apart: 3, of which 3 were waited for; matrix products, arithmetic and copies ran while one was open for 1% of the time, Pallas kernels for 0%

commit v1 on v0

--- a/solution.py
+++ b/solution.py
@@ -32,7 +32,12 @@
     emb = (proj / norm).astype(jnp.bfloat16)
     embed = emb.shape[1]
     own_cols = lax.dynamic_slice_in_dim(emb, part * width, width, 0)
-    columns = lax.all_gather(own_cols, "dp", axis=0, tiled=True)
+    ring = [own_cols]
+    for hop in range(15):
+        ring.append(lax.ppermute(ring[-1], "dp", [(dev, (dev + 1) % 16) for dev in range(16)]))
+    columns = jnp.roll(
+        jnp.concatenate(ring[::-1], axis=0), (lax.axis_index("dp") + 1) * ring[0].shape[0], axis=0
+    )
     col_total = columns.shape[0]
     shard_ids = jnp.arange(shards, dtype=jnp.int32)
     my_block = jnp.sum(jnp.where(shard_ids == shard, window, 0))

time: 235 us -> 295 us (1.26)
  waiting for transfers between devices: 94.9 us -> 177 us
  blocking collectives: 108 us -> 86.3 us
    ppermute x0 -> x15, waiting for transfers between devices: none -> 77.9 us  [on_device(): lax.ppermute(ring[-1], 'dp', [(dev, (dev + 1) % 16) for dev in range(16)])]
    all_gather x1 -> x0, blocking collectives: 18.1 us -> none  [on_device(): columns = lax.all_gather(own_cols, 'dp', axis=0, tiled=True)]
    psum x1, waiting for transfers between devices: 19.6 us -> 24.4 us  [on_device(): lax.psum(jnp.dot(hidden, w_out, preferred_element_type=jnp.float32), 'mp')]
    all_gather x1, blocking collectives: 21.7 us -> 18.3 us  [on_device(): piece = lax.all_gather(anchors, 'dp', axis=0, tiled=True)]
    unnamed x25 -> x56, local copies, waits for them, and re-layouts: 7.68 us -> 7.35 us
  transfers between devices with their start and end apart: 3 -> 18, of which waited for: 3 -> 17; matrix products, arithmetic and copies ran while one was open for 1% -> 1% of each run, Pallas kernels for 0% -> 0%
where the time goes in v1:
time: 295 us
  waiting for transfers between devices  177 us (60%)
  blocking collectives  86.3 us (29%)
  between operations  15.3 us (5%)
  local copies, waits for them, and re-layouts  7.53 us (3%)
  matrix products  4.86 us (2%)
  other arithmetic  3.56 us (1%)
    ppermute x15, waiting for transfers between devices, on_device(): lax.ppermute(ring[-1], 'dp', [(dev, (dev + 1) % 16) for dev in range(16)])  77.9 us
    psum x1, waiting for transfers between devices, on_device(): lax.psum((grad_w_in, grad_b_in, grad_w_out), 'dp')  57.8 us
    psum x1, blocking collectives, on_device(): lax.psum((grad_w_in, grad_b_in, grad_w_out), 'dp')  33.6 us
    unnamed x1, blocking collectives  29.5 us
    psum x1, waiting for transfers between devices, on_device(): lax.psum(jnp.dot(hidden, w_out, preferred_element_type=jnp.float32), 'mp')  24.4 us
    all_gather x1, blocking collectives, on_device(): piece = lax.all_gather(anchors, 'dp', axis=0, tiled=True)  18.3 us
    psum x1, waiting for transfers between devices, on_device(): grad_emb = lax.psum(row_placed + placed, 'mp') * (INV_TEMP / anchor_all)  17.1 us
    unnamed x56, local copies, waits for them, and re-layouts  7.35 us
  transfers between devices with their start and end apart: 18, of which 17 were waited for; matrix products, arithmetic and copies ran while one was open for 1% of the time, Pallas kernels for 0%

profile of v1, /device:TPU:0, one launch (start us, length us, event | category | flops | bytes accessed | tf_op | source)
XLA Modules:
  0.0 295.1 jit_solution(12894953340705878339)
XLA Ops:
  7.2 0.0 copy-start
  7.2 0.0 all-reduce.7.cloned.1.call-start
  7.2 0.9 copy-done
  8.1 1.1 multiply_convert_fusion
  9.3 0.8 fusion.61
  10.0 0.0 all-reduce.7.cloned.1.call-update
  10.1 0.0 all-reduce.9.cloned.1.call-start
  10.1 24.4 %all-reduce.7.cloned.1.call-done = f32[128,128]{1,0:T(8,128)} async-done(((f32[128,128]{1,0:T(8,128)}), f32[128,128]{1,0:T(8,128)}) %all-reduce.7.cloned.1.call-update) | async-done | bytes 65552 | tf_op jit(solution)/shard_map/psum | solution.py:30
  34.5 1.0 multiply_reduce_fusion.1
  35.6 0.1 fusion.60
  35.7 0.0 copy-start.7
  35.7 0.1 collective-permute-start
  35.8 5.8 %collective-permute-done = bf16[64,128]{1,0:T(8,128)(2,1)S(1)} collective-permute-done((bf16[64,128]{1,0:T(8,128)(2,1)S(1)}, bf16[64,128]{1,0:T(8,128)(2,1)S(1)}, u32[]{:S(2)}, u32[]{:S(2)}) %collective-permute-start) | collective-permute-done | bytes 16416 | tf_op jit(solution)/shard_map/ppermute | solution.py:37
  41.6 0.0 collective-permute-start.1
  41.6 5.9 %collective-permute-done.1 = bf16[64,128]{1,0:T(8,128)(2,1)S(1)} collective-permute-done((bf16[64,128]{1,0:T(8,128)(2,1)S(1)}, bf16[64,128]{1,0:T(8,128)(2,1)S(1)}, u32[]{:S(2)}, u32[]{:S(2)}) %collective-permute-start.1) | collective-permute-done | bytes 16416 | tf_op jit(solution)/shard_map/ppermute | solution.py:37
  47.5 0.0 collective-permute-start.2
  47.5 5.9 %collective-permute-done.2 = bf16[64,128]{1,0:T(8,128)(2,1)S(1)} collective-permute-done((bf16[64,128]{1,0:T(8,128)(2,1)S(1)}, bf16[64,128]{1,0:T(8,128)(2,1)S(1)}, u32[]{:S(2)}, u32[]{:S(2)}) %collective-permute-start.2) | collective-permute-done | bytes 16416 | tf_op jit(solution)/shard_map/ppermute | solution.py:37
  53.3 0.0 collective-permute-start.3
  53.3 5.9 %collective-permute-done.3 = bf16[64,128]{1,0:T(8,128)(2,1)S(1)} collective-permute-done((bf16[64,128]{1,0:T(8,128)(2,1)S(1)}, bf16[64,128]{1,0:T(8,128)(2,1)S(1)}, u32[]{:S(2)}, u32[]{:S(2)}) %collective-permute-start.3) | collective-permute-done | bytes 16416 | tf_op jit(solution)/shard_map/ppermute | solution.py:37
  59.2 0.0 collective-permute-start.4
  59.2 5.9 %collective-permute-done.4 = bf16[64,128]{1,0:T(8,128)(2,1)S(1)} collective-permute-done((bf16[64,128]{1,0:T(8,128)(2,1)S(1)}, bf16[64,128]{1,0:T(8,128)(2,1)S(1)}, u32[]{:S(2)}, u32[]{:S(2)}) %collective-permute-start.4) | collective-permute-done | bytes 16416 | tf_op jit(solution)/shard_map/ppermute | solution.py:37
  65.1 0.0 collective-permute-start.5
  65.1 5.9 %collective-permute-done.5 = bf16[64,128]{1,0:T(8,128)(2,1)S(1)} collective-permute-done((bf16[64,128]{1,0:T(8,128)(2,1)S(1)}, bf16[64,128]{1,0:T(8,128)(2,1)S(1)}, u32[]{:S(2)}, u32[]{:S(2)}) %collective-permute-start.5) | collective-permute-done | bytes 16416 | tf_op jit(solution)/shard_map/ppermute | solution.py:37
  70.9 5.9 %collective-permute-done.6 = bf16[64,128]{1,0:T(8,128)(2,1)S(1)} collective-permute-done((bf16[64,128]{1,0:T(8,128)(2,1)S(1)}, bf16[64,128]{1,0:T(8,128)(2,1)S(1)}, u32[]{:S(2)}, u32[]{:S(2)}) %collective-permute-start.6) | collective-permute-done | bytes 16416 | tf_op jit(solution)/shard_map/ppermute | solution.py:37
  76.8 0.1 select_reduce_fusion
  76.9 5.8 %collective-permute-done.7 = bf16[64,128]{1,0:T(8,128)(2,1)S(1)} collective-permute-done((bf16[64,128]{1,0:T(8,128)(2,1)S(1)}, bf16[64,128]{1,0:T(8,128)(2,1)S(1)}, u32[]{:S(2)}, u32[]{:S(2)}) %collective-permute-start.7) | collective-permute-done | bytes 16416 | tf_op jit(solution)/shard_map/ppermute | solution.py:37
  82.7 5.8 %collective-permute-done.8 = bf16[64,128]{1,0:T(8,128)(2,1)S(1)} collective-permute-done((bf16[64,128]{1,0:T(8,128)(2,1)S(1)}, bf16[64,128]{1,0:T(8,128)(2,1)S(1)}, u32[]{:S(2)}, u32[]{:S(2)}) %collective-permute-start.8) | collective-permute-done | bytes 16416 | tf_op jit(solution)/shard_map/ppermute | solution.py:37
  88.5 0.6 fusion.54
  89.1 5.2 %collective-permute-done.9 = bf16[64,128]{1,0:T(8,128)(2,1)S(1)} collective-permute-done((bf16[64,128]{1,0:T(8,128)(2,1)S(1)}, bf16[64,128]{1,0:T(8,128)(2,1)S(1)}, u32[]{:S(2)}, u32[]{:S(2)}) %collective-permute-start.9) | collective-permute-done | bytes 16416 | tf_op jit(solution)/shard_map/ppermute | solution.py:37
  95.0 5.2 %collective-permute-done.10 = bf16[64,128]{1,0:T(8,128)(2,1)S(1)} collective-permute-done((bf16[64,128]{1,0:T(8,128)(2,1)S(1)}, bf16[64,128]{1,0:T(8,128)(2,1)S(1)}, u32[]{:S(2)}, u32[]{:S(2)}) %collective-permute-start.10) | collective-permute-done | bytes 16416 | tf_op jit(solution)/shard_map/ppermute | solution.py:37
  100.2 5.9 %collective-permute-done.11 = bf16[64,128]{1,0:T(8,128)(2,1)S(1)} collective-permute-done((bf16[64,128]{1,0:T(8,128)(2,1)S(1)}, bf16[64,128]{1,0:T(8,128)(2,1)S(1)}, u32[]{:S(2)}, u32[]{:S(2)}) %collective-permute-start.11) | collective-permute-done | bytes 16416 | tf_op jit(solution)/shard_map/ppermute | solution.py:37
  106.1 0.0 collective-permute-start.12
  106.1 0.7 copy-done.8
  106.8 0.1 dynamic_slice.37
  106.8 0.1 dynamic_slice.36
  106.9 0.7 copy-done.9
  107.6 0.6 dynamic-slice.3
  108.8 3.2 %collective-permute-done.12 = bf16[64,128]{1,0:T(8,128)(2,1)S(1)} collective-permute-done((bf16[64,128]{1,0:T(8,128)(2,1)S(1)}, bf16[64,128]{1,0:T(8,128)(2,1)S(1)}, u32[]{:S(2)}, u32[]{:S(2)}) %collective-permute-start.12) | collective-permute-done | bytes 16416 | tf_op jit(solution)/shard_map/ppermute | solution.py:37
  112.0 0.0 collective-permute-start.13
  112.0 5.9 %collective-permute-done.13 = bf16[64,128]{1,0:T(8,128)(2,1)S(1)} collective-permute-done((bf16[64,128]{1,0:T(8,128)(2,1)S(1)}, bf16[64,128]{1,0:T(8,128)(2,1)S(1)}, u32[]{:S(2)}, u32[]{:S(2)}) %collective-permute-start.13) | collective-permute-done | bytes 16416 | tf_op jit(solution)/shard_map/ppermute | solution.py:37
  117.8 0.0 collective-permute-start.14
  117.8 18.3 %all_gather.6 = bf16[512,128]{1,0:T(8,128)(2,1)S(1)} all-gather(bf16[32,128]{1,0:T(8,128)(2,1)S(1)} %constant_dynamic-slice_fusion.1), channel_id=1, replica_groups=mesh['dp'=16,'mp'=2] {'dp'}, dimensions={0}, use_global_device_ids=true | all-gather | bytes 139264 | tf_op jit(solution)/shard_map/all_gather | solution.py:91
  136.6 0.3 fusion.13
  136.9 4.9 %all-reduce.2 = (f32[32]{0:T(128)S(1)}, f32[32]{0:T(128)S(1)}) all-reduce(f32[32]{0:T(128)S(1)} %get-tuple-element.70, f32[32]{0:T(128)S(1)} %get-tuple-element.69), channel_id=1, replica_groups=mesh['dp'=16,'mp'=2] {'mp'}, use_global_device_ids=true, to_apply=%region_6.7 | all-reduce | flops 64 | bytes 512 | tf_op jit(solution)/shard_map/psum | solution.py:69
  141.8 0.2 dynamic-update-slice.1
  142.0 29.5 %all-reduce = f32[512]{0:T(512)S(1)} all-reduce(f32[512]{0:T(512)S(1)} %dynamic-update-slice.1), channel_id=1, replica_groups=mesh['dp'=16,'mp'=2] {'dp'}, use_global_device_ids=true, to_apply=%add | all-reduce | flops 512 | bytes 4096
  171.5 0.2 convolution_dynamic-update-slice_fusion
  171.7 0.3 fusion.10
  172.1 0.6 copy-done.3
  172.7 0.0 all-reduce.9.cloned.1.call-update
  172.7 0.0 all-reduce.11.cloned.1.call-start
  172.8 17.1 %all-reduce.9.cloned.1.call-done = f32[128,128]{1,0:T(8,128)} async-done(((f32[128,128]{1,0:T(8,128)}), f32[128,128]{1,0:T(8,128)}) %all-reduce.9.cloned.1.call-update) | async-done | bytes 65552 | tf_op jit(solution)/shard_map/psum | solution.py:121
  189.9 1.1 multiply_reduce_fusion
  191.0 0.1 divide_convert_fusion
  191.1 0.9 fusion.62
  191.9 0.2 convert_reduce_fusion
  192.1 0.7 copy-done.5
  192.8 1.0 convolution_bitcast_fusion
  193.9 0.0 all-reduce.11.cloned.1.call-update
  193.9 0.5 add_subtract_fusion
  194.4 33.6 %psum.54 = f32[256]{0:T(256)} all-reduce(f32[256]{0:T(256)S(1)} %get-tuple-element.87), channel_id=1, replica_groups=mesh['dp'=16,'mp'=2] {'dp'}, use_global_device_ids=true, to_apply=%region_12.13 | all-reduce | flops 256 | bytes 2048 | tf_op jit(solution)/shard_map/psum | solution.py:134
  228.0 57.8 %all-reduce.11.cloned.1.call-done = (f32[512,256]{0,1:T(8,128)}, f32[256,128]{1,0:T(8,128)}) async-done(((f32[512,256]{0,1:T(8,128)}, f32[256,128]{1,0:T(8,128)}), (f32[512,256]{0,1:T(8,128)}, f32[256,128]{1,0:T(8,128)})) %all-reduce.11.cloned.1.call-update) | async-done | bytes 655376 | tf_op jit(solution)/shard_map/psum | solution.py:134
  285.8 2.1 copy.11
  287.9 0.7 copy.50
  (62 shorter events, 0.4 us)
Async XLA Ops:
  7.2 1.0 copy-start
  7.2 2.1 copy-start.6
  7.2 27.3 %all-reduce.7.cloned.1.call-start = ((), (), s32[]{:S(2)}) async-start(), calls=%async_computation | async-start | bytes 131072 | tf_op jit(solution)/shard_map/psum | solution.py:30
  10.1 179.8 %all-reduce.9.cloned.1.call-start = ((), (), s32[]{:S(2)}) async-start(), calls=%async_computation.1 | async-start | bytes 131072 | tf_op jit(solution)/shard_map/psum | solution.py:121
  34.5 1.0 copy-start.1
  35.7 41.1 %copy-start.7 = (s32[16]{0:T(128)S(1)}, s32[16]{0:T(128)}, u32[]{:S(2)}) copy-start(s32[16]{0:T(128)} %param.11) | copy-start | bytes 196
  35.7 5.9 %collective-permute-start = (bf16[64,128]{1,0:T(8,128)(2,1)S(1)}, bf16[64,128]{1,0:T(8,128)(2,1)S(1)}, u32[]{:S(2)}, u32[]{:S(2)}) collective-permute-start(bf16[64,128]{1,0:T(8,128)(2,1)S(1)} %constant_dynamic-slice_fusion), channel_id=1, source_target_pairs={{0,2},{2,4},{4,6},{6,8},{8,10},{10,12},{12,14},{14,16},{16,18},{18... | collective-permute-start | bytes 49160 | tf_op jit(solution)/shard_map/ppermute | solution.py:37
  41.6 5.9 %collective-permute-start.1 = (bf16[64,128]{1,0:T(8,128)(2,1)S(1)}, bf16[64,128]{1,0:T(8,128)(2,1)S(1)}, u32[]{:S(2)}, u32[]{:S(2)}) collective-permute-start(bf16[64,128]{1,0:T(8,128)(2,1)S(1)} %collective-permute-done), channel_id=1, source_target_pairs={{0,2},{2,4},{4,6},{6,8},{8,10},{10,12},{12,14},{14,16},{16,18},{18... | collective-permute-start | bytes 49160 | tf_op jit(solution)/shard_map/ppermute | solution.py:37
  47.5 5.9 %collective-permute-start.2 = (bf16[64,128]{1,0:T(8,128)(2,1)S(1)}, bf16[64,128]{1,0:T(8,128)(2,1)S(1)}, u32[]{:S(2)}, u32[]{:S(2)}) collective-permute-start(bf16[64,128]{1,0:T(8,128)(2,1)S(1)} %collective-permute-done.1), channel_id=1, source_target_pairs={{0,2},{2,4},{4,6},{6,8},{8,10},{10,12},{12,14},{14,16},{16,18},{18... | collective-permute-start | bytes 49160 | tf_op jit(solution)/shard_map/ppermute | solution.py:37
  53.3 5.9 %collective-permute-start.3 = (bf16[64,128]{1,0:T(8,128)(2,1)S(1)}, bf16[64,128]{1,0:T(8,128)(2,1)S(1)}, u32[]{:S(2)}, u32[]{:S(2)}) collective-permute-start(bf16[64,128]{1,0:T(8,128)(2,1)S(1)} %collective-permute-done.2), channel_id=1, source_target_pairs={{0,2},{2,4},{4,6},{6,8},{8,10},{10,12},{12,14},{14,16},{16,18},{18... | collective-permute-start | bytes 49160 | tf_op jit(solution)/shard_map/ppermute | solution.py:37
  59.2 5.9 %collective-permute-start.4 = (bf16[64,128]{1,0:T(8,128)(2,1)S(1)}, bf16[64,128]{1,0:T(8,128)(2,1)S(1)}, u32[]{:S(2)}, u32[]{:S(2)}) collective-permute-start(bf16[64,128]{1,0:T(8,128)(2,1)S(1)} %collective-permute-done.3), channel_id=1, source_target_pairs={{0,2},{2,4},{4,6},{6,8},{8,10},{10,12},{12,14},{14,16},{16,18},{18... | collective-permute-start | bytes 49160 | tf_op jit(solution)/shard_map/ppermute | solution.py:37
  65.1 5.9 %collective-permute-start.5 = (bf16[64,128]{1,0:T(8,128)(2,1)S(1)}, bf16[64,128]{1,0:T(8,128)(2,1)S(1)}, u32[]{:S(2)}, u32[]{:S(2)}) collective-permute-start(bf16[64,128]{1,0:T(8,128)(2,1)S(1)} %collective-permute-done.4), channel_id=1, source_target_pairs={{0,2},{2,4},{4,6},{6,8},{8,10},{10,12},{12,14},{14,16},{16,18},{18... | collective-permute-start | bytes 49160 | tf_op jit(solution)/shard_map/ppermute | solution.py:37
  70.9 5.9 %collective-permute-start.6 = (bf16[64,128]{1,0:T(8,128)(2,1)S(1)}, bf16[64,128]{1,0:T(8,128)(2,1)S(1)}, u32[]{:S(2)}, u32[]{:S(2)}) collective-permute-start(bf16[64,128]{1,0:T(8,128)(2,1)S(1)} %collective-permute-done.5), channel_id=1, source_target_pairs={{0,2},{2,4},{4,6},{6,8},{8,10},{10,12},{12,14},{14,16},{16,18},{18... | collective-permute-start | bytes 49160 | tf_op jit(solution)/shard_map/ppermute | solution.py:37
  76.8 5.9 %collective-permute-start.7 = (bf16[64,128]{1,0:T(8,128)(2,1)S(1)}, bf16[64,128]{1,0:T(8,128)(2,1)S(1)}, u32[]{:S(2)}, u32[]{:S(2)}) collective-permute-start(bf16[64,128]{1,0:T(8,128)(2,1)S(1)} %collective-permute-done.6), channel_id=1, source_target_pairs={{0,2},{2,4},{4,6},{6,8},{8,10},{10,12},{12,14},{14,16},{16,18},{18... | collective-permute-start | bytes 49160 | tf_op jit(solution)/shard_map/ppermute | solution.py:37
  82.6 5.9 %collective-permute-start.8 = (bf16[64,128]{1,0:T(8,128)(2,1)S(1)}, bf16[64,128]{1,0:T(8,128)(2,1)S(1)}, u32[]{:S(2)}, u32[]{:S(2)}) collective-permute-start(bf16[64,128]{1,0:T(8,128)(2,1)S(1)} %collective-permute-done.7), channel_id=1, source_target_pairs={{0,2},{2,4},{4,6},{6,8},{8,10},{10,12},{12,14},{14,16},{16,18},{18... | collective-permute-start | bytes 49160 | tf_op jit(solution)/shard_map/ppermute | solution.py:37
  88.5 5.9 %collective-permute-start.9 = (bf16[64,128]{1,0:T(8,128)(2,1)S(1)}, bf16[64,128]{1,0:T(8,128)(2,1)S(1)}, u32[]{:S(2)}, u32[]{:S(2)}) collective-permute-start(bf16[64,128]{1,0:T(8,128)(2,1)S(1)} %collective-permute-done.8), channel_id=1, source_target_pairs={{0,2},{2,4},{4,6},{6,8},{8,10},{10,12},{12,14},{14,16},{16,18},{18... | collective-permute-start | bytes 49160 | tf_op jit(solution)/shard_map/ppermute | solution.py:37
  94.4 5.9 %collective-permute-start.10 = (bf16[64,128]{1,0:T(8,128)(2,1)S(1)}, bf16[64,128]{1,0:T(8,128)(2,1)S(1)}, u32[]{:S(2)}, u32[]{:S(2)}) collective-permute-start(bf16[64,128]{1,0:T(8,128)(2,1)S(1)} %collective-permute-done.9), channel_id=1, source_target_pairs={{0,2},{2,4},{4,6},{6,8},{8,10},{10,12},{12,14},{14,16},{16,18},{18... | collective-permute-start | bytes 49160 | tf_op jit(solution)/shard_map/ppermute | solution.py:37
  100.2 5.9 %collective-permute-start.11 = (bf16[64,128]{1,0:T(8,128)(2,1)S(1)}, bf16[64,128]{1,0:T(8,128)(2,1)S(1)}, u32[]{:S(2)}, u32[]{:S(2)}) collective-permute-start(bf16[64,128]{1,0:T(8,128)(2,1)S(1)} %collective-permute-done.10), channel_id=1, source_target_pairs={{0,2},{2,4},{4,6},{6,8},{8,10},{10,12},{12,14},{14,16},{16,18},{18... | collective-permute-start | bytes 49160 | tf_op jit(solution)/shard_map/ppermute | solution.py:37
  106.1 5.9 %collective-permute-start.12 = (bf16[64,128]{1,0:T(8,128)(2,1)S(1)}, bf16[64,128]{1,0:T(8,128)(2,1)S(1)}, u32[]{:S(2)}, u32[]{:S(2)}) collective-permute-start(bf16[64,128]{1,0:T(8,128)(2,1)S(1)} %collective-permute-done.11), channel_id=1, source_target_pairs={{0,2},{2,4},{4,6},{6,8},{8,10},{10,12},{12,14},{14,16},{16,18},{18... | collective-permute-start | bytes 49160 | tf_op jit(solution)/shard_map/ppermute | solution.py:37
  106.1 0.7 copy-start.8
  106.9 0.7 copy-start.9
  112.0 5.9 %collective-permute-start.13 = (bf16[64,128]{1,0:T(8,128)(2,1)S(1)}, bf16[64,128]{1,0:T(8,128)(2,1)S(1)}, u32[]{:S(2)}, u32[]{:S(2)}) collective-permute-start(bf16[64,128]{1,0:T(8,128)(2,1)S(1)} %collective-permute-done.12), channel_id=1, source_target_pairs={{0,2},{2,4},{4,6},{6,8},{8,10},{10,12},{12,14},{14,16},{16,18},{18... | collective-permute-start | bytes 49160 | tf_op jit(solution)/shard_map/ppermute | solution.py:37
  117.8 18.3 %collective-permute-start.14 = (bf16[64,128]{1,0:T(8,128)(2,1)S(1)}, bf16[64,128]{1,0:T(8,128)(2,1)S(1)}, u32[]{:S(2)}, u32[]{:S(2)}) collective-permute-start(bf16[64,128]{1,0:T(8,128)(2,1)S(1)} %collective-permute-done.13), channel_id=1, source_target_pairs={{0,2},{2,4},{4,6},{6,8},{8,10},{10,12},{12,14},{14,16},{16,18},{18... | collective-permute-start | bytes 49160 | tf_op jit(solution)/shard_map/ppermute | solution.py:37
  172.1 0.6 copy-start.3
  172.7 113.1 %all-reduce.11.cloned.1.call-start = ((), (), s32[]{:S(2)}) async-start(), calls=%async_computation.2 | async-start | bytes 1310720 | tf_op jit(solution)/shard_map/psum | solution.py:134
  189.9 1.1 copy-start.2
  191.9 0.9 copy-start.5
  285.8 2.1 copy-start.4
Sparse Core Ops, SparseCore 0:
  10.8 23.6 all-reduce.6
  172.9 16.9 all-reduce.8
  194.0 91.7 all-reduce.10
